TPU v7x, 512 devices: a whole 4x8x8 slice. The times are simulated.
512 devices in a mesh: dp: 32 (over x, y), segment: 2 (over core), mp: 8 (over z).
Axes of the slice: x: 4, y: 8, z: 8, core: 2. Of those that a mesh axis runs over, the one named last changes fastest.
Arguments:
- frames: bfloat16 [2, 8192, 1280], P(None, ('dp', 'mp')), may hold values from -8 to 8
- dec_states: bfloat16 [2, 2048, 1280], P(None, 'dp'), may hold values from -8 to 8
- out_grad: bfloat16 [2, 2048, 1280], P(None, 'dp'), may hold values from -3 to 3
- frame_lengths: int32 [2, 32, 4], P(None, 'dp'), may hold values from 1 to 128, 256 in all within a row
- token_lengths: int32 [2, 32, 4], P(None, 'dp'), may hold values from 1 to 32, 64 in all within a row
- weights: bfloat16 [2, 4, 1024, 1280], P('segment', None, 'mp'), may hold values from -1 to 1
- norm_gains: float32 [3, 1280], replicated, may hold values from 0.25 to 1.75
- norm_biases: float32 [3, 1280], replicated, may hold values from -2 to 2
Outputs:
- gradient: float32 [2, 3, 1024, 1280], P('segment', None, 'mp')
Inputs may be any that keep to these rules, and one draw needn't show every extreme that they name: `frame_lengths`: the 4 utterance lengths of each micro-batch and group sum to 256. `token_lengths`: the 4 token counts of each micro-batch and group sum to 64.
All inputs are finite; a program needn't handle non-finite values.
Results may differ from a plain program's by a relative error of at most 0.04.
Values may be sent and summed in bfloat16 or wider, within the bound.
No kernel may reach another device: no remote copies, remote signals or barrier semaphores. Data moves between devices by JAX's collectives and lax.ppermute only.
A program may use at most 64 MiB of HBM per device.

v0:
```python
import math
import jax
import jax.numpy as jnp
from jax import lax
from jax.sharding import PartitionSpec as P

HS = 64
EPSILON = 1e-05
ROWS_DIMS = (((0,), (0,)), ((), ()))
FEAT_DIMS = (((1,), (1,)), ((), ()))


def layer_norm(values, norm_gain, offset):
    center = values - jnp.mean(values, axis=-1, keepdims=True)
    variance = jnp.mean(center * center, axis=-1, keepdims=True)
    return center * lax.rsqrt(variance + EPSILON) * norm_gain + offset


def norm_backward(grad_out, values, norm_gain):
    center = values - jnp.mean(values, axis=-1, keepdims=True)
    variance = jnp.mean(center * center, axis=-1, keepdims=True)
    inverse = lax.rsqrt(variance + EPSILON)
    normed = center * inverse
    scaled = grad_out * norm_gain
    return inverse * (
        scaled
        - jnp.mean(scaled, axis=-1, keepdims=True)
        - normed * jnp.mean(scaled * normed, axis=-1, keepdims=True)
    )


def utterance_ids(lengths, row_count):
    bounds = jnp.cumsum(lengths, dtype=jnp.int32)
    places = jnp.arange(row_count, dtype=jnp.int32)
    return jnp.sum((places[:, None] >= bounds[None, :]).astype(jnp.int32), axis=1)


def project(row_block, matrix):
    return lax.dot_general(row_block, matrix, FEAT_DIMS, preferred_element_type=jnp.float32).astype(
        jnp.bfloat16
    )


def outer_rows(left_rows, right_rows):
    return lax.dot_general(left_rows, right_rows, ROWS_DIMS, preferred_element_type=jnp.float32)


def split_heads(row_block):
    return row_block.reshape(row_block.shape[0], -1, HS)


def attend(queries, key_rows, value_rows, allowed):
    scaling = 1.0 / math.sqrt(HS)
    scores = (
        jnp.einsum(
            "qhd,khd->hqk",
            split_heads(queries),
            split_heads(key_rows),
            preferred_element_type=jnp.float32,
        )
        * scaling
    )
    scores = jnp.where(allowed[None], scores, -1e30)
    highest = jnp.max(scores, axis=-1, keepdims=True)
    raised = jnp.exp(scores - highest)
    attn_probs = raised / jnp.sum(raised, axis=-1, keepdims=True)
    context = jnp.einsum(
        "hqk,khd->qhd",
        attn_probs.astype(jnp.bfloat16),
        split_heads(value_rows),
        preferred_element_type=jnp.float32,
    )
    return (context.reshape(queries.shape[0], -1).astype(jnp.bfloat16), attn_probs)


def attend_backward(queries, key_rows, value_rows, attn_probs, grad_context):
    scaling = 1.0 / math.sqrt(HS)
    grad_heads = split_heads(grad_context)
    grad_probs = jnp.einsum(
        "qhd,khd->hqk", grad_heads, split_heads(value_rows), preferred_element_type=jnp.float32
    )
    grad_scores = (
        attn_probs * (grad_probs - jnp.sum(grad_probs * attn_probs, axis=-1, keepdims=True))
    ).astype(jnp.bfloat16)
    key_grad = (
        jnp.einsum(
            "hqk,qhd->khd", grad_scores, split_heads(queries), preferred_element_type=jnp.float32
        )
        * scaling
    )
    key_grad = key_grad.reshape(key_rows.shape[0], -1).astype(jnp.bfloat16)
    value_grad = jnp.einsum(
        "hqk,qhd->khd",
        attn_probs.astype(jnp.bfloat16),
        grad_heads,
        preferred_element_type=jnp.float32,
    )
    value_grad = value_grad.reshape(key_rows.shape[0], -1).astype(jnp.bfloat16)
    return (key_grad, value_grad)


def spread(block, axis):
    size = lax.axis_size(axis)
    return lax.all_to_all(jnp.broadcast_to(block[None], (size,) + block.shape), axis, 0, 0)


def share_sum(blocks, axis):
    return jnp.sum(lax.all_to_all(blocks, axis, 0, 0).astype(jnp.float32), axis=0)


def swap(block):
    return lax.ppermute(block, "segment", [(0, 1), (1, 0)])


def to_chunks(block, parts):
    high, wide = (block.shape[0] // 8, block.shape[1] // 128)
    tiles = block.reshape(high, 8, wide, 128).transpose(0, 2, 1, 3).reshape(-1, 8, 128)
    each = -(-tiles.shape[0] // parts)
    tiles = jnp.pad(tiles, ((0, each * parts - tiles.shape[0]), (0, 0), (0, 0)))
    return tiles.reshape(parts, each, 8, 128)


def from_chunks(chunks, rows, cols):
    high, wide = (rows // 8, cols // 128)
    tiles = chunks.reshape(-1, 8, 128)[: high * wide]
    return tiles.reshape(high, wide, 8, 128).transpose(0, 2, 1, 3).reshape(rows, cols)


def shards(
    frames, dec_states, out_grad, frame_lengths, token_lengths, weights, norm_gains, norm_biases
):
    core = lax.axis_index("segment")
    first = core == 0
    own = weights[0]
    shard_rows, features = frames.shape[1:]
    mp = lax.axis_size("mp")
    dp = lax.axis_size("dp")
    head_cols = own.shape[1]
    rows = shard_rows * mp
    half = features // 2

    def mine(array):
        return lax.dynamic_index_in_dim(array, core, 0, keepdims=False)

    inputs = mine(frames)
    tokens = mine(dec_states)
    upstream = mine(out_grad)
    frame_ids = utterance_ids(mine(frame_lengths)[0], rows)
    token_ids = utterance_ids(mine(token_lengths)[0], tokens.shape[0])
    out_sent = lax.ppermute(own[3, :, half:], "segment", [(0, 1)])
    out_part = jnp.where(first, own[3, :, :half], out_sent)
    out_part = lax.all_gather(out_part, "mp", axis=0, tiled=True)
    out_rest = swap(out_part)
    enc_full = spread(inputs, "mp").reshape(rows, features)
    other = swap(own)
    enc = jnp.where(first, own, other)
    dec = jnp.where(first, other, own)
    normed = layer_norm(enc_full.astype(jnp.float32), norm_gains[0], norm_biases[0]).astype(
        jnp.bfloat16
    )
    queries = project(normed, enc[0])
    key_rows = project(normed, enc[1])
    value_rows = project(normed, enc[2])
    context, probs = attend(queries, key_rows, value_rows, frame_ids[:, None] == frame_ids[None, :])
    context_full = spread(context, "mp").transpose(1, 0, 2).reshape(rows, mp * head_cols)
    out_mine = jnp.dot(context_full, out_part, preferred_element_type=jnp.float32)
    out_other = jnp.dot(context_full, out_rest, preferred_element_type=jnp.float32)
    summed = jnp.concatenate(
        [jnp.where(first, out_mine, out_other), jnp.where(first, out_other, out_mine)], axis=1
    )
    states_full = (enc_full.astype(jnp.float32) + summed).astype(jnp.bfloat16)
    states = lax.dynamic_slice_in_dim(states_full, lax.axis_index("mp") * shard_rows, shard_rows, 0)
    state_normed = layer_norm(
        states_full.astype(jnp.float32), norm_gains[2], norm_biases[2]
    ).astype(jnp.bfloat16)
    token_normed = layer_norm(tokens.astype(jnp.float32), norm_gains[1], norm_biases[1]).astype(
        jnp.bfloat16
    )
    dec_queries = project(token_normed, dec[0])
    dec_keys = project(state_normed, dec[1])
    dec_values = project(state_normed, dec[2])
    dec_context, dec_probs = attend(
        dec_queries, dec_keys, dec_values, token_ids[:, None] == frame_ids[None, :]
    )
    grad_context = project(upstream, dec[3])
    dec_key_grad, dec_value_grad = attend_backward(
        dec_queries, dec_keys, dec_values, dec_probs, grad_context
    )
    partial = (
        jnp.dot(dec_key_grad, dec[1], preferred_element_type=jnp.float32)
        + jnp.dot(dec_value_grad, dec[2], preferred_element_type=jnp.float32)
    ).astype(jnp.bfloat16)

    def combine(term):
        left, right = (term[:, :half], term[:, half:])
        sent = swap(jnp.where(first, right, left).astype(jnp.bfloat16))
        return (jnp.where(first, left, right) + sent.astype(jnp.float32)).astype(jnp.bfloat16)

    def reduce_groups(term):
        total = share_sum(to_chunks(term, dp), "dp").astype(jnp.bfloat16)
        return from_chunks(spread(total, "dp"), 3 * head_cols, half)

    dec_term = jnp.concatenate(
        [
            outer_rows(dec_key_grad, state_normed),
            outer_rows(dec_value_grad, state_normed),
            outer_rows(dec_context, upstream),
        ]
    )
    pieces = lax.all_to_all(partial.reshape(mp, shard_rows, features), "mp", 0, 0)
    pieces, dec_part = lax.optimization_barrier((pieces, combine(dec_term)))
    dec_total = lax.psum(dec_part, "dp")
    summed = jnp.sum(pieces.astype(jnp.float32), axis=0)
    grads = norm_backward(summed, states.astype(jnp.float32), norm_gains[2]).astype(jnp.bfloat16)
    grads_full = spread(grads, "mp").reshape(rows, features)
    att_grad = project(grads_full, enc[3])
    enc_key_grad, enc_value_grad = attend_backward(queries, key_rows, value_rows, probs, att_grad)
    enc_term = jnp.concatenate(
        [
            outer_rows(enc_key_grad, normed),
            outer_rows(enc_value_grad, normed),
            outer_rows(context, grads_full),
        ]
    )
    enc_total = reduce_groups(combine(enc_term))
    kept = jnp.where(first, enc_total, dec_total)
    got = swap(jnp.where(first, dec_total, enc_total))
    gradient = jnp.concatenate(
        [jnp.where(first, kept, got), jnp.where(first, got, kept)], axis=1
    ).astype(jnp.float32)
    return gradient.reshape(1, 3, head_cols, features)


def solution(mesh):
    placed = (
        P(None, ("dp", "mp"), None),
        P(None, "dp", None),
        P(None, "dp", None),
        P(None, "dp", None),
        P(None, "dp", None),
        P("segment", None, "mp", None),
        P(),
        P(),
    )
    return jax.shard_map(
        shards,
        mesh=mesh,
        in_specs=placed,
        out_specs=P("segment", None, "mp", None),
        check_vma=False,
    )
```

profile of v0, /device:TPU:1, one launch (start us, length us, event | category | flops | bytes accessed | tf_op | source)
XLA Modules:
  0.0 379.2 jit_solution(9192799755561751875)
XLA Ops:
  8.5 10.9 %all-to-all-start = ((bf16[8,32,1280]{2,1,0:T(8,128)(2,1)}), bf16[8,32,1280]{2,1,0:T(8,128)(2,1)S(1)}, u32[]{:S(2)}, u32[]{:S(2)}) async-start(bf16[8,32,1280]{2,1,0:T(8,128)(2,1)} %broadcast_in_dim.31), calls=%async_computation | async-start | bytes 1310720 | tf_op jit(solution)/shard_map/all_to_all | solution.py:104
  19.4 2.9 collective-permute-start
  27.3 12.8 %all-to-all-done = bf16[8,32,1280]{2,1,0:T(8,128)(2,1)S(1)} async-done(((bf16[8,32,1280]{2,1,0:T(8,128)(2,1)}), bf16[8,32,1280]{2,1,0:T(8,128)(2,1)S(1)}, u32[]{:S(2)}, u32[]{:S(2)}) %all-to-all-start) | async-done | bytes 655392 | tf_op jit(solution)/shard_map/all_to_all | solution.py:104
  41.4 1.5 broadcast_select_fusion.1
  44.4 23.2 %all-gather.2.cloned.1.call-done = bf16[1024,640]{1,0:T(8,128)(2,1)} async-done(((bf16[128,640]{1,0:T(8,128)(2,1)}), bf16[1024,640]{1,0:T(8,128)(2,1)}) %all-gather.2.cloned.1.call-update) | async-done | bytes 1310736 | tf_op jit(solution)/shard_map/all_gather | solution.py:152
  67.6 7.2 %collective-permute-start.2 = (bf16[1024,640]{1,0:T(8,128)(2,1)}, bf16[1024,640]{1,0:T(8,128)(2,1)}, u32[]{:S(2)}, u32[]{:S(2)}) collective-permute-start(bf16[1024,640]{1,0:T(8,128)(2,1)} %all-gather.2.cloned.1.call-done), channel_id=1, source_target_pairs={{0,8},{8,0},{1,9},{9,1},{2,10},{10,2},{3,11},{11,3},{4,12},{12,4},... | collective-permute-start | bytes 3932168 | tf_op jit(solution)/shard_map/ppermute | solution.py:112
  77.4 3.9 %all-to-all-start.1 = ((bf16[8,256,128]{1,2,0:T(8,128)(2,1)}), bf16[8,256,128]{1,2,0:T(8,128)(2,1)S(1)}, u32[]{:S(2)}, u32[]{:S(2)}) async-start(bf16[8,256,128]{1,2,0:T(8,128)(2,1)} %broadcast_in_dim.34), calls=%async_computation.1 | async-start | bytes 1048576 | tf_op jit(solution)/shard_map/all_to_all | solution.py:104
  87.1 12.2 %all-to-all-done.1 = bf16[8,256,128]{1,2,0:T(8,128)(2,1)S(1)} async-done(((bf16[8,256,128]{1,2,0:T(8,128)(2,1)}), bf16[8,256,128]{1,2,0:T(8,128)(2,1)S(1)}, u32[]{:S(2)}, u32[]{:S(2)}) %all-to-all-start.1) | async-done | bytes 524320 | tf_op jit(solution)/shard_map/all_to_all | solution.py:104
  99.3 1.9 fusion.72
  101.2 1.9 broadcast_select_fusion.7
  107.3 2.4 fusion.25
  114.6 2.2 fusion.2
  116.8 3.5 all-to-all-start.2
  120.3 1.6 pad_maximum_fusion
  122.0 2.4 collective-permute-start.3
  126.9 14.1 %all-to-all-done.2 = bf16[8,32,1280]{2,1,0:T(8,128)(2,1)S(1)} async-done(((bf16[8,32,1280]{2,1,0:T(8,128)(2,1)}), bf16[8,32,1280]{2,1,0:T(8,128)(2,1)S(1)}, u32[]{:S(2)}, u32[]{:S(2)}) %all-to-all-start.2) | async-done | bytes 655392 | tf_op jit(solution)/shard_map/all_to_all | solution.py:210
  141.5 22.3 %all_to_all.30 = bf16[8,32,1280]{2,1,0:T(8,128)(2,1)S(1)} all-to-all(bf16[8,32,1280]{2,1,0:T(8,128)(2,1)S(1)} %broadcast_in_dim.37), channel_id=1, replica_groups=mesh['dp'=32,'segment'=2,'mp'=8] {'mp'}, dimensions={0} | all-to-all | bytes 1310720 | tf_op jit(solution)/shard_map/all_to_all | solution.py:104
  169.5 3.2 collective-permute-start.4
  174.4 23.2 %all_to_all.31 = bf16[32,8,8,128]{3,2,1,0:T(8,128)(2,1)S(1)} all-to-all(bf16[32,8,8,128]{3,2,1,0:T(8,128)(2,1)S(1)} %bitcast.176), channel_id=1, replica_groups=mesh['dp'=32,'segment'=2,'mp'=8] {'dp'}, dimensions={0} | all-to-all | bytes 1048576 | tf_op jit(solution)/shard_map/all_to_all | solution.py:108
  198.6 8.1 %all-to-all-start.5 = ((bf16[32,8,8,128]{3,2,1,0:T(8,128)(2,1)}), bf16[32,8,8,128]{3,2,1,0:T(8,128)(2,1)S(1)}, u32[]{:S(2)}, u32[]{:S(2)}) async-start(bf16[32,8,8,128]{3,2,1,0:T(8,128)(2,1)} %broadcast_in_dim.42), calls=%async_computation.5 | async-start | bytes 1048576 | tf_op jit(solution)/shard_map/all_to_all | solution.py:104
  207.5 13.3 %all-to-all-done.5 = bf16[32,8,8,128]{3,2,1,0:T(8,128)(2,1)S(1)} async-done(((bf16[32,8,8,128]{3,2,1,0:T(8,128)(2,1)}), bf16[32,8,8,128]{3,2,1,0:T(8,128)(2,1)S(1)}, u32[]{:S(2)}, u32[]{:S(2)}) %all-to-all-start.5) | async-done | bytes 524320 | tf_op jit(solution)/shard_map/all_to_all | solution.py:104
  220.8 140.2 %all-reduce.3.cloned.1.call-done = bf16[384,640]{1,0:T(8,128)(2,1)} async-done(((bf16[384,640]{1,0:T(8,128)(2,1)}), bf16[384,640]{1,0:T(8,128)(2,1)}) %all-reduce.3.cloned.1.call-update) | async-done | bytes 491536 | tf_op jit(solution)/shard_map/psum | solution.py:212
  361.1 8.2 %collective-permute-start.5 = (bf16[384,640]{1,0:T(8,128)(2,1)S(1)}, bf16[384,640]{1,0:T(8,128)(2,1)S(1)}, u32[]{:S(2)}, u32[]{:S(2)}) collective-permute-start(bf16[384,640]{1,0:T(8,128)(2,1)S(1)} %broadcast_select_fusion.4), channel_id=1, source_target_pairs={{0,8},{8,0},{1,9},{9,1},{2,10},{10,2},{3,11},{11,3},{4,12},{12,4},... | collective-permute-start | bytes 1474568 | tf_op jit(solution)/shard_map/ppermute | solution.py:112
  369.3 1.5 collective-permute-done.5
  (150 shorter events, 40.5 us)
Async XLA Ops:
  6.5 78.3 %copy-start = (bf16[2,64,1280]{2,1,0:T(8,128)(2,1)S(1)}, bf16[2,64,1280]{2,1,0:T(8,128)(2,1)}, u32[]{:S(2)}) copy-start(bf16[2,64,1280]{2,1,0:T(8,128)(2,1)} %param.10) | copy-start | bytes 983044
  6.5 12.9 %copy-start.4 = (bf16[1,4,128,1280]{3,2,1,0:T(8,128)(2,1)S(1)}, bf16[1,4,128,1280]{3,2,1,0:T(8,128)(2,1)}, u32[]{:S(2)}) copy-start(bf16[1,4,128,1280]{3,2,1,0:T(8,128)(2,1)} %param.13) | copy-start | bytes 3932164
  6.5 17.1 %copy-start.20 = (s32[2,1,4]{2,1,0:T(1,128)S(1)}, s32[2,1,4]{2,1,0:T(1,128)}, u32[]{:S(2)}) copy-start(s32[2,1,4]{2,1,0:T(1,128)} %param.11) | copy-start | bytes 100
  6.5 17.1 %copy-start.21 = (s32[2,1,4]{2,1,0:T(1,128)S(1)}, s32[2,1,4]{2,1,0:T(1,128)}, u32[]{:S(2)}) copy-start(s32[2,1,4]{2,1,0:T(1,128)} %param.12) | copy-start | bytes 100
  6.5 17.4 %copy-start.8 = (bf16[2,64,1280]{2,1,0:T(8,128)(2,1)S(1)}, bf16[2,64,1280]{2,1,0:T(8,128)(2,1)}, u32[]{:S(2)}) copy-start(bf16[2,64,1280]{2,1,0:T(8,128)(2,1)} %param.9) | copy-start | bytes 983044
  7.6 18.3 %copy-start.14 = (f32[3,1280]{1,0:T(4,128)S(1)}, f32[3,1280]{1,0:T(4,128)}, u32[]{:S(2)}) copy-start(f32[3,1280]{1,0:T(4,128)} %param.15) | copy-start | bytes 46084
  7.6 18.3 %copy-start.15 = (f32[3,1280]{1,0:T(4,128)S(1)}, f32[3,1280]{1,0:T(4,128)}, u32[]{:S(2)}) copy-start(f32[3,1280]{1,0:T(4,128)} %param.14) | copy-start | bytes 46084
  8.5 31.6 %all-to-all-start = ((bf16[8,32,1280]{2,1,0:T(8,128)(2,1)}), bf16[8,32,1280]{2,1,0:T(8,128)(2,1)S(1)}, u32[]{:S(2)}, u32[]{:S(2)}) async-start(bf16[8,32,1280]{2,1,0:T(8,128)(2,1)} %broadcast_in_dim.31), calls=%async_computation | async-start | bytes 1310720 | tf_op jit(solution)/shard_map/all_to_all | solution.py:104
  19.3 48.2 %all-gather.2.cloned.1.call-start = ((), (), s32[]{:S(2)}) async-start(), calls=%async_computation.6 | async-start | bytes 1474560 | tf_op jit(solution)/shard_map/all_gather | solution.py:152
  19.4 21.6 %collective-permute-start = (bf16[4,128,1280]{2,1,0:T(8,128)(2,1)S(1)}, bf16[4,128,1280]{2,1,0:T(8,128)(2,1)}, u32[]{:S(2)}, u32[]{:S(2)}) collective-permute-start(bf16[4,128,1280]{2,1,0:T(8,128)(2,1)S(1)} %bitcast.177), channel_id=1, source_target_pairs={{0,8},{8,0},{1,9},{9,1},{2,10},{10,2},{3,11},{11,3},{4,12},{12,4},... | collective-permute-start | bytes 3932168 | tf_op jit(solution)/shard_map/ppermute | solution.py:112
  22.3 4.3 %collective-permute-start.1 = (bf16[128,640]{1,0:T(8,128)(2,1)S(1)}, bf16[128,640]{1,0:T(8,128)(2,1)S(1)}, u32[]{:S(2)}, u32[]{:S(2)}) collective-permute-start(bf16[128,640]{1,0:T(8,128)(2,1)S(1)} %slice_bitcast_fusion.18), channel_id=1, source_target_pairs={{0,8},{1,9},{2,10},{3,11},{4,12},{5,13},{6,14},{7,15},{16,24},{17,... | collective-permute-start | bytes 491528 | tf_op jit(solution)/shard_map/ppermute | solution.py:150
  25.3 50.7 %copy-start.10 = (pred[256,256]{0,1:T(8,128)(4,1)}, pred[256,256]{0,1:T(8,128)(4,1)S(1)}, u32[]{:S(2)}) copy-start(pred[256,256]{0,1:T(8,128)(4,1)S(1)} %broadcast_compare_fusion) | copy-start | bytes 196612
  42.9 41.9 %copy-start.2 = (bf16[4,128,1280]{2,1,0:T(8,128)(2,1)}, bf16[4,128,1280]{2,1,0:T(8,128)(2,1)S(1)}, u32[]{:S(2)}) copy-start(bf16[4,128,1280]{2,1,0:T(8,128)(2,1)S(1)} %get-tuple-element.22) | copy-start | bytes 3932164
  43.3 32.7 %copy-start.22 = (bf16[256,128]{0,1:T(8,128)(2,1)}, bf16[256,128]{0,1:T(8,128)(2,1)S(1)}, u32[]{:S(2)}) copy-start(bf16[256,128]{0,1:T(8,128)(2,1)S(1)} %convolution_convert_fusion.5) | copy-start | bytes 196612
  44.0 32.5 %copy-start.24 = (bf16[256,128]{0,1:T(8,128)(2,1)}, bf16[256,128]{0,1:T(8,128)(2,1)S(1)}, u32[]{:S(2)}) copy-start(bf16[256,128]{0,1:T(8,128)(2,1)S(1)} %convolution_convert_fusion.6) | copy-start | bytes 196612
  44.3 32.2 %copy-start.26 = (bf16[256,128]{0,1:T(8,128)(2,1)}, bf16[256,128]{0,1:T(8,128)(2,1)S(1)}, u32[]{:S(2)}) copy-start(bf16[256,128]{0,1:T(8,128)(2,1)S(1)} %convolution_convert_fusion.4) | copy-start | bytes 196612
  67.6 31.7 %collective-permute-start.2 = (bf16[1024,640]{1,0:T(8,128)(2,1)}, bf16[1024,640]{1,0:T(8,128)(2,1)}, u32[]{:S(2)}, u32[]{:S(2)}) collective-permute-start(bf16[1024,640]{1,0:T(8,128)(2,1)} %all-gather.2.cloned.1.call-done), channel_id=1, source_target_pairs={{0,8},{8,0},{1,9},{9,1},{2,10},{10,2},{3,11},{11,3},{4,12},{12,4},... | collective-permute-start | bytes 3932168 | tf_op jit(solution)/shard_map/ppermute | solution.py:112
  77.4 21.9 %all-to-all-start.1 = ((bf16[8,256,128]{1,2,0:T(8,128)(2,1)}), bf16[8,256,128]{1,2,0:T(8,128)(2,1)S(1)}, u32[]{:S(2)}, u32[]{:S(2)}) async-start(bf16[8,256,128]{1,2,0:T(8,128)(2,1)} %broadcast_in_dim.34), calls=%async_computation.1 | async-start | bytes 1048576 | tf_op jit(solution)/shard_map/all_to_all | solution.py:104
  116.8 24.2 %all-to-all-start.2 = ((bf16[8,32,1280]{2,1,0:T(8,128)(2,1)}), bf16[8,32,1280]{2,1,0:T(8,128)(2,1)S(1)}, u32[]{:S(2)}, u32[]{:S(2)}) async-start(bf16[8,32,1280]{2,1,0:T(8,128)(2,1)} %bitcast.37), calls=%async_computation.2 | async-start | bytes 1310720 | tf_op jit(solution)/shard_map/all_to_all | solution.py:210
  122.0 3.9 %collective-permute-start.3 = (bf16[384,640]{1,0:T(8,128)(2,1)S(1)}, bf16[384,640]{1,0:T(8,128)(2,1)S(1)}, u32[]{:S(2)}, u32[]{:S(2)}) collective-permute-start(bf16[384,640]{1,0:T(8,128)(2,1)S(1)} %select_convert_fusion.1), channel_id=1, source_target_pairs={{0,8},{8,0},{1,9},{9,1},{2,10},{10,2},{3,11},{11,3},{4,12},{12,4},... | collective-permute-start | bytes 1474568 | tf_op jit(solution)/shard_map/ppermute | solution.py:112
  169.5 4.7 %collective-permute-start.4 = (bf16[384,640]{1,0:T(8,128)(2,1)S(1)}, bf16[384,640]{1,0:T(8,128)(2,1)S(1)}, u32[]{:S(2)}, u32[]{:S(2)}) collective-permute-start(bf16[384,640]{1,0:T(8,128)(2,1)S(1)} %select_convert_fusion), channel_id=1, source_target_pairs={{0,8},{8,0},{1,9},{9,1},{2,10},{10,2},{3,11},{11,3},{4,12},{12,4},... | collective-permute-start | bytes 1474568 | tf_op jit(solution)/shard_map/ppermute | solution.py:112
  198.6 22.2 %all-to-all-start.5 = ((bf16[32,8,8,128]{3,2,1,0:T(8,128)(2,1)}), bf16[32,8,8,128]{3,2,1,0:T(8,128)(2,1)S(1)}, u32[]{:S(2)}, u32[]{:S(2)}) async-start(bf16[32,8,8,128]{3,2,1,0:T(8,128)(2,1)} %broadcast_in_dim.42), calls=%async_computation.5 | async-start | bytes 1048576 | tf_op jit(solution)/shard_map/all_to_all | solution.py:104
  206.7 154.3 %all-reduce.3.cloned.1.call-start = ((), (), s32[]{:S(2)}) async-start(), calls=%async_computation.7 | async-start | bytes 983040 | tf_op jit(solution)/shard_map/psum | solution.py:212
  361.1 9.7 %collective-permute-start.5 = (bf16[384,640]{1,0:T(8,128)(2,1)S(1)}, bf16[384,640]{1,0:T(8,128)(2,1)S(1)}, u32[]{:S(2)}, u32[]{:S(2)}) collective-permute-start(bf16[384,640]{1,0:T(8,128)(2,1)S(1)} %broadcast_select_fusion.4), channel_id=1, source_target_pairs={{0,8},{8,0},{1,9},{9,1},{2,10},{10,2},{3,11},{11,3},{4,12},{12,4},... | collective-permute-start | bytes 1474568 | tf_op jit(solution)/shard_map/ppermute | solution.py:112
  (20 other events, 37.7 us)
Sparse Core Ops, SparseCore 0:
  27.4 40.0 all-gather.1
  210.9 150.0 all-reduce.2
where the time goes:
time: 380 us; the launch traced here: 379 us
  waiting for transfers between devices  220 us (58%)
  starting transfers between devices  51.7 us (14%)
  blocking collectives  45.5 us (12%)
  matrix products  25.7 us (7%)
  between operations  14 us (4%)
  other arithmetic  13.8 us (4%)
  local copies, waits for them, and re-layouts  8.81 us (2%)
    psum x1, waiting for transfers between devices, shards(): dec_total = lax.psum(dec_part, 'dp')  140 us
    all_to_all x3, waiting for transfers between devices, spread(): lax.all_to_all(jnp.broadcast_to(block[None], (size,) + block.shape), axis...  38.3 us
    ppermute x5, starting transfers between devices, swap(): return lax.ppermute(block, 'segment', [(0, 1), (1, 0)])  23.9 us
    all_to_all x1, blocking collectives, share_sum(): lax.all_to_all(blocks, axis, 0, 0).astype(jnp.float32)  23.2 us
    all_gather x1, waiting for transfers between devices, shards(): out_part = lax.all_gather(out_part, 'mp', axis=0, tiled=True)  23.2 us
    all_to_all x3, starting transfers between devices, spread(): lax.all_to_all(jnp.broadcast_to(block[None], (size,) + block.shape), axis...  22.8 us
    all_to_all x1, blocking collectives, spread(): lax.all_to_all(jnp.broadcast_to(block[None], (size,) + block.shape), axis...  22.3 us
    all_to_all x1, waiting for transfers between devices, shards(): lax.all_to_all(partial.reshape(mp, shard_rows, features), 'mp', 0, 0)  14.1 us
  transfers between devices with their start and end apart: 12, of which 9 were waited for; matrix products, arithmetic and copies ran while one was open for 5% of the time, Pallas kernels for 0%

commit v1 on v0

--- a/solution.py
+++ b/solution.py
@@ -149,7 +149,10 @@
     token_ids = utterance_ids(mine(token_lengths)[0], tokens.shape[0])
     out_sent = lax.ppermute(own[3, :, half:], "segment", [(0, 1)])
     out_part = jnp.where(first, own[3, :, :half], out_sent)
-    out_part = lax.all_gather(out_part, "mp", axis=0, tiled=True)
+    assign_panel_for = lambda view: jnp.concatenate(
+        lax.all_to_all(jnp.stack([view for _ in range(lax.axis_size("mp"))]), "mp", 0, 0), axis=0
+    )
+    out_part = assign_panel_for(out_part)
     out_rest = swap(out_part)
     enc_full = spread(inputs, "mp").reshape(rows, features)
     other = swap(own)

time: 380 us -> 388 us (1.021)
    all_to_all x0 -> x1, waiting for transfers between devices: none -> 29.5 us  [shards(): lax.all_to_all(jnp.stack([view for _ in range(lax.axis_size('mp'))]), 'mp...]
    all_gather x1 -> x0, waiting for transfers between devices: 23.2 us -> none  [shards(): out_part = lax.all_gather(out_part, 'mp', axis=0, tiled=True)]
    ppermute x5, starting transfers between devices: 23.9 us -> 19 us  [swap(): return lax.ppermute(block, 'segment', [(0, 1), (1, 0)])]
  transfers between devices with their start and end apart: 12 -> 12, of which waited for: 9 -> 9; matrix products, arithmetic and copies ran while one was open for 5% -> 7% of each run, Pallas kernels for 0% -> 0%
where the time goes in v1:
time: 388 us; the launch traced here: 386 us
  waiting for transfers between devices  223 us (57%)
  starting transfers between devices  50 us (13%)
  blocking collectives  45.9 us (12%)
  matrix products  26.6 us (7%)
  other arithmetic  15.5 us (4%)
  between operations  14 us (4%)
  local copies, waits for them, and re-layouts  11.6 us (3%)
    psum x1, waiting for transfers between devices, shards(): dec_total = lax.psum(dec_part, 'dp')  140 us
    all_to_all x3, waiting for transfers between devices, spread(): lax.all_to_all(jnp.broadcast_to(block[None], (size,) + block.shape), axis...  35.2 us
    all_to_all x1, waiting for transfers between devices, shards(): lax.all_to_all(jnp.stack([view for _ in range(lax.axis_size('mp'))]), 'mp...  29.5 us
    all_to_all x1, blocking collectives, share_sum(): lax.all_to_all(blocks, axis, 0, 0).astype(jnp.float32)  23.6 us
    all_to_all x3, starting transfers between devices, spread(): lax.all_to_all(jnp.broadcast_to(block[None], (size,) + block.shape), axis...  22.5 us
    all_to_all x1, blocking collectives, spread(): lax.all_to_all(jnp.broadcast_to(block[None], (size,) + block.shape), axis...  22.3 us
    ppermute x5, starting transfers between devices, swap(): return lax.ppermute(block, 'segment', [(0, 1), (1, 0)])  19 us
    all_to_all x1, waiting for transfers between devices, shards(): lax.all_to_all(partial.reshape(mp, shard_rows, features), 'mp', 0, 0)  14.2 us
  transfers between devices with their start and end apart: 12, of which 9 were waited for; matrix products, arithmetic and copies ran while one was open for 7% of the time, Pallas kernels for 0%

profile of v1, /device:TPU:1, one launch (start us, length us, event | category | flops | bytes accessed | tf_op | source)
XLA Modules:
  0.0 386.4 jit_solution(17197426798169045118)
XLA Ops:
  8.4 10.9 %all-to-all-start = ((bf16[8,32,1280]{2,1,0:T(8,128)(2,1)}), bf16[8,32,1280]{2,1,0:T(8,128)(2,1)S(1)}, u32[]{:S(2)}, u32[]{:S(2)}) async-start(bf16[8,32,1280]{2,1,0:T(8,128)(2,1)} %broadcast_in_dim.31), calls=%async_computation | async-start | bytes 1310720 | tf_op jit(solution)/shard_map/all_to_all | solution.py:104
  19.3 2.9 collective-permute-start
  28.3 11.7 %all-to-all-done = bf16[8,32,1280]{2,1,0:T(8,128)(2,1)S(1)} async-done(((bf16[8,32,1280]{2,1,0:T(8,128)(2,1)}), bf16[8,32,1280]{2,1,0:T(8,128)(2,1)S(1)}, u32[]{:S(2)}, u32[]{:S(2)}) %all-to-all-start) | async-done | bytes 655392 | tf_op jit(solution)/shard_map/all_to_all | solution.py:104
  41.2 3.6 all-to-all-start.2
  45.6 2.9 broadcast_select_fusion.1
  50.0 29.5 %all-to-all-done.2 = bf16[8,128,640]{2,1,0:T(8,128)(2,1)S(1)} async-done(((bf16[8,128,640]{2,1,0:T(8,128)(2,1)}), bf16[8,128,640]{2,1,0:T(8,128)(2,1)S(1)}, u32[]{:S(2)}, u32[]{:S(2)}) %all-to-all-start.2) | async-done | bytes 1310752 | tf_op jit(solution)/shard_map/all_to_all | solution.py:153
  79.5 2.4 collective-permute-start.2
  84.6 3.5 all-to-all-start.1
  89.4 1.9 convolution_convert_fusion.11
  92.7 1.8 convolution_convert_fusion.10
  96.0 10.2 %all-to-all-done.1 = bf16[8,256,128]{2,1,0:T(8,128)(2,1)S(1)} async-done(((bf16[8,256,128]{2,1,0:T(8,128)(2,1)}), bf16[8,256,128]{2,1,0:T(8,128)(2,1)S(1)}, u32[]{:S(2)}, u32[]{:S(2)}) %all-to-all-start.1) | async-done | bytes 524320 | tf_op jit(solution)/shard_map/all_to_all | solution.py:104
  107.1 2.2 fusion.73
  114.1 2.4 fusion.25
  121.4 2.2 fusion.2
  123.6 3.5 all-to-all-start.3
  128.9 2.3 collective-permute-start.3
  133.7 14.2 %all-to-all-done.3 = bf16[8,32,1280]{2,1,0:T(8,128)(2,1)S(1)} async-done(((bf16[8,32,1280]{2,1,0:T(8,128)(2,1)}), bf16[8,32,1280]{2,1,0:T(8,128)(2,1)S(1)}, u32[]{:S(2)}, u32[]{:S(2)}) %all-to-all-start.3) | async-done | bytes 655392 | tf_op jit(solution)/shard_map/all_to_all | solution.py:213
  148.3 22.3 %all_to_all.35 = bf16[8,32,1280]{2,1,0:T(8,128)(2,1)S(1)} all-to-all(bf16[8,32,1280]{2,1,0:T(8,128)(2,1)S(1)} %broadcast_in_dim.37), channel_id=1, replica_groups=mesh['dp'=32,'segment'=2,'mp'=8] {'mp'}, dimensions={0} | all-to-all | bytes 1310720 | tf_op jit(solution)/shard_map/all_to_all | solution.py:104
  176.3 3.2 collective-permute-start.4
  181.2 23.6 %all_to_all.36 = bf16[32,8,8,128]{3,2,1,0:T(8,128)(2,1)S(1)} all-to-all(bf16[32,8,8,128]{3,2,1,0:T(8,128)(2,1)S(1)} %bitcast.182), channel_id=1, replica_groups=mesh['dp'=32,'segment'=2,'mp'=8] {'dp'}, dimensions={0} | all-to-all | bytes 1048576 | tf_op jit(solution)/shard_map/all_to_all | solution.py:108
  205.8 8.1 %all-to-all-start.6 = ((bf16[32,8,8,128]{3,2,1,0:T(8,128)(2,1)}), bf16[32,8,8,128]{3,2,1,0:T(8,128)(2,1)S(1)}, u32[]{:S(2)}, u32[]{:S(2)}) async-start(bf16[32,8,8,128]{3,2,1,0:T(8,128)(2,1)} %broadcast_in_dim.42), calls=%async_computation.6 | async-start | bytes 1048576 | tf_op jit(solution)/shard_map/all_to_all | solution.py:104
  214.7 13.3 %all-to-all-done.6 = bf16[32,8,8,128]{3,2,1,0:T(8,128)(2,1)S(1)} async-done(((bf16[32,8,8,128]{3,2,1,0:T(8,128)(2,1)}), bf16[32,8,8,128]{3,2,1,0:T(8,128)(2,1)S(1)}, u32[]{:S(2)}, u32[]{:S(2)}) %all-to-all-start.6) | async-done | bytes 524320 | tf_op jit(solution)/shard_map/all_to_all | solution.py:104
  228.1 140.2 %all-reduce.3.cloned.1.call-done = bf16[384,640]{1,0:T(8,128)(2,1)} async-done(((bf16[384,640]{1,0:T(8,128)(2,1)}), bf16[384,640]{1,0:T(8,128)(2,1)}) %all-reduce.3.cloned.1.call-update) | async-done | bytes 491536 | tf_op jit(solution)/shard_map/psum | solution.py:215
  368.3 8.2 %collective-permute-start.5 = (bf16[384,640]{1,0:T(8,128)(2,1)S(1)}, bf16[384,640]{1,0:T(8,128)(2,1)S(1)}, u32[]{:S(2)}, u32[]{:S(2)}) collective-permute-start(bf16[384,640]{1,0:T(8,128)(2,1)S(1)} %broadcast_select_fusion.4), channel_id=1, source_target_pairs={{0,8},{8,0},{1,9},{9,1},{2,10},{10,2},{3,11},{11,3},{4,12},{12,4},... | collective-permute-start | bytes 1474568 | tf_op jit(solution)/shard_map/ppermute | solution.py:112
  (150 shorter events, 45.4 us)
Async XLA Ops:
  6.5 86.2 %copy-start = (bf16[2,64,1280]{2,1,0:T(8,128)(2,1)S(1)}, bf16[2,64,1280]{2,1,0:T(8,128)(2,1)}, u32[]{:S(2)}) copy-start(bf16[2,64,1280]{2,1,0:T(8,128)(2,1)} %param.10) | copy-start | bytes 983044
  6.5 17.8 %copy-start.19 = (s32[2,1,4]{2,1,0:T(1,128)S(1)}, s32[2,1,4]{2,1,0:T(1,128)}, u32[]{:S(2)}) copy-start(s32[2,1,4]{2,1,0:T(1,128)} %param.11) | copy-start | bytes 100
  6.5 17.8 %copy-start.20 = (s32[2,1,4]{2,1,0:T(1,128)S(1)}, s32[2,1,4]{2,1,0:T(1,128)}, u32[]{:S(2)}) copy-start(s32[2,1,4]{2,1,0:T(1,128)} %param.12) | copy-start | bytes 100
  6.5 18.1 %copy-start.7 = (bf16[2,64,1280]{2,1,0:T(8,128)(2,1)S(1)}, bf16[2,64,1280]{2,1,0:T(8,128)(2,1)}, u32[]{:S(2)}) copy-start(bf16[2,64,1280]{2,1,0:T(8,128)(2,1)} %param.9) | copy-start | bytes 983044
  7.5 19.2 %copy-start.13 = (f32[3,1280]{1,0:T(4,128)S(1)}, f32[3,1280]{1,0:T(4,128)}, u32[]{:S(2)}) copy-start(f32[3,1280]{1,0:T(4,128)} %param.15) | copy-start | bytes 46084
  7.5 19.2 %copy-start.14 = (f32[3,1280]{1,0:T(4,128)S(1)}, f32[3,1280]{1,0:T(4,128)}, u32[]{:S(2)}) copy-start(f32[3,1280]{1,0:T(4,128)} %param.14) | copy-start | bytes 46084
  8.4 31.6 %all-to-all-start = ((bf16[8,32,1280]{2,1,0:T(8,128)(2,1)}), bf16[8,32,1280]{2,1,0:T(8,128)(2,1)S(1)}, u32[]{:S(2)}, u32[]{:S(2)}) async-start(bf16[8,32,1280]{2,1,0:T(8,128)(2,1)} %broadcast_in_dim.31), calls=%async_computation | async-start | bytes 1310720 | tf_op jit(solution)/shard_map/all_to_all | solution.py:104
  19.3 26.4 %collective-permute-start = (bf16[4,128,1280]{2,1,0:T(8,128)(2,1)}, bf16[4,128,1280]{2,1,0:T(8,128)(2,1)}, u32[]{:S(2)}, u32[]{:S(2)}) collective-permute-start(bf16[4,128,1280]{2,1,0:T(8,128)(2,1)} %bitcast.2), channel_id=1, source_target_pairs={{0,8},{8,0},{1,9},{9,1},{2,10},{10,2},{3,11},{11,3},{4,12},{12,4},... | collective-permute-start | bytes 3932168 | tf_op jit(solution)/shard_map/ppermute | solution.py:112
  23.1 4.3 %collective-permute-start.1 = (bf16[128,640]{1,0:T(8,128)(2,1)S(1)}, bf16[128,640]{1,0:T(8,128)(2,1)S(1)}, u32[]{:S(2)}, u32[]{:S(2)}) collective-permute-start(bf16[128,640]{1,0:T(8,128)(2,1)S(1)} %slice_bitcast_fusion.18), channel_id=1, source_target_pairs={{0,8},{1,9},{2,10},{3,11},{4,12},{5,13},{6,14},{7,15},{16,24},{17,... | collective-permute-start | bytes 491528 | tf_op jit(solution)/shard_map/ppermute | solution.py:150
  26.1 57.0 %copy-start.9 = (pred[256,256]{0,1:T(8,128)(4,1)}, pred[256,256]{0,1:T(8,128)(4,1)S(1)}, u32[]{:S(2)}) copy-start(pred[256,256]{0,1:T(8,128)(4,1)S(1)} %broadcast_compare_fusion) | copy-start | bytes 196612
  41.2 38.3 %all-to-all-start.2 = ((bf16[8,128,640]{2,1,0:T(8,128)(2,1)}), bf16[8,128,640]{2,1,0:T(8,128)(2,1)S(1)}, u32[]{:S(2)}, u32[]{:S(2)}) async-start(bf16[8,128,640]{2,1,0:T(8,128)(2,1)} %stack.2), calls=%async_computation.2 | async-start | bytes 2621440 | tf_op jit(solution)/shard_map/all_to_all | solution.py:153
  48.9 34.1 %copy-start.21 = (bf16[256,128]{0,1:T(8,128)(2,1)}, bf16[256,128]{0,1:T(8,128)(2,1)S(1)}, u32[]{:S(2)}) copy-start(bf16[256,128]{0,1:T(8,128)(2,1)S(1)} %convolution_convert_fusion.5) | copy-start | bytes 196612
  49.6 34.0 %copy-start.23 = (bf16[256,128]{0,1:T(8,128)(2,1)}, bf16[256,128]{0,1:T(8,128)(2,1)S(1)}, u32[]{:S(2)}) copy-start(bf16[256,128]{0,1:T(8,128)(2,1)S(1)} %convolution_convert_fusion.6) | copy-start | bytes 196612
  50.0 33.6 %copy-start.25 = (bf16[256,128]{0,1:T(8,128)(2,1)}, bf16[256,128]{0,1:T(8,128)(2,1)S(1)}, u32[]{:S(2)}) copy-start(bf16[256,128]{0,1:T(8,128)(2,1)S(1)} %convolution_convert_fusion.4) | copy-start | bytes 196612
  79.5 4.1 %copy-start.1 = (bf16[8,128,640]{2,1,0:T(8,128)(2,1)}, bf16[8,128,640]{2,1,0:T(8,128)(2,1)S(1)}, u32[]{:S(2)}) copy-start(bf16[8,128,640]{2,1,0:T(8,128)(2,1)S(1)} %all-to-all-done.2) | copy-start | bytes 3932164
  79.5 27.6 %collective-permute-start.2 = (bf16[1024,640]{1,0:T(8,128)(2,1)S(1)}, bf16[1024,640]{1,0:T(8,128)(2,1)}, u32[]{:S(2)}, u32[]{:S(2)}) collective-permute-start(bf16[1024,640]{1,0:T(8,128)(2,1)S(1)} %bitcast.175), channel_id=1, source_target_pairs={{0,8},{8,0},{1,9},{9,1},{2,10},{10,2},{3,11},{11,3},{4,12},{12,4},... | collective-permute-start | bytes 3932168 | tf_op jit(solution)/shard_map/ppermute | solution.py:112
  84.6 21.5 %all-to-all-start.1 = ((bf16[8,256,128]{2,1,0:T(8,128)(2,1)}), bf16[8,256,128]{2,1,0:T(8,128)(2,1)S(1)}, u32[]{:S(2)}, u32[]{:S(2)}) async-start(bf16[8,256,128]{2,1,0:T(8,128)(2,1)} %broadcast_in_dim.34), calls=%async_computation.1 | async-start | bytes 1048576 | tf_op jit(solution)/shard_map/all_to_all | solution.py:104
  123.6 24.2 %all-to-all-start.3 = ((bf16[8,32,1280]{2,1,0:T(8,128)(2,1)}), bf16[8,32,1280]{2,1,0:T(8,128)(2,1)S(1)}, u32[]{:S(2)}, u32[]{:S(2)}) async-start(bf16[8,32,1280]{2,1,0:T(8,128)(2,1)} %bitcast.38), calls=%async_computation.3 | async-start | bytes 1310720 | tf_op jit(solution)/shard_map/all_to_all | solution.py:213
  128.9 3.8 collective-permute-start.3
  176.3 4.7 %collective-permute-start.4 = (bf16[384,640]{1,0:T(8,128)(2,1)S(1)}, bf16[384,640]{1,0:T(8,128)(2,1)S(1)}, u32[]{:S(2)}, u32[]{:S(2)}) collective-permute-start(bf16[384,640]{1,0:T(8,128)(2,1)S(1)} %select_convert_fusion), channel_id=1, source_target_pairs={{0,8},{8,0},{1,9},{9,1},{2,10},{10,2},{3,11},{11,3},{4,12},{12,4},... | collective-permute-start | bytes 1474568 | tf_op jit(solution)/shard_map/ppermute | solution.py:112
  205.8 22.2 %all-to-all-start.6 = ((bf16[32,8,8,128]{3,2,1,0:T(8,128)(2,1)}), bf16[32,8,8,128]{3,2,1,0:T(8,128)(2,1)S(1)}, u32[]{:S(2)}, u32[]{:S(2)}) async-start(bf16[32,8,8,128]{3,2,1,0:T(8,128)(2,1)} %broadcast_in_dim.42), calls=%async_computation.6 | async-start | bytes 1048576 | tf_op jit(solution)/shard_map/all_to_all | solution.py:104
  214.0 154.3 %all-reduce.3.cloned.1.call-start = ((), (), s32[]{:S(2)}) async-start(), calls=%async_computation.7 | async-start | bytes 983040 | tf_op jit(solution)/shard_map/psum | solution.py:215
  368.3 9.8 %copy-start.5 = (bf16[384,640]{1,0:T(8,128)(2,1)S(1)}, bf16[384,640]{1,0:T(8,128)(2,1)}, u32[]{:S(2)}) copy-start(bf16[384,640]{1,0:T(8,128)(2,1)} %all-reduce.3.cloned.1.call-done) | copy-start | bytes 1474564
  368.3 9.7 %collective-permute-start.5 = (bf16[384,640]{1,0:T(8,128)(2,1)S(1)}, bf16[384,640]{1,0:T(8,128)(2,1)S(1)}, u32[]{:S(2)}, u32[]{:S(2)}) collective-permute-start(bf16[384,640]{1,0:T(8,128)(2,1)S(1)} %broadcast_select_fusion.4), channel_id=1, source_target_pairs={{0,8},{8,0},{1,9},{9,1},{2,10},{10,2},{3,11},{11,3},{4,12},{12,4},... | collective-permute-start | bytes 1474568 | tf_op jit(solution)/shard_map/ppermute | solution.py:112
  (19 other events, 29.0 us)
Sparse Core Ops, SparseCore 0:
  218.2 150.0 all-reduce.2
